TPU v7x, 256 devices: a whole 4x4x8 slice. The times are simulated.
256 devices in a mesh: row: 16 (over x_hi, z), col: 16 (over y, x_lo, core).
Axes of the slice: x: 4 (x_hi: 2, x_lo: 2; x = x_hi * 2 + x_lo), y: 4, z: 8, core: 2. Of those that a mesh axis runs over, the one named last changes fastest.
Arguments:
- objective: float32 [256, 32768], P('row', 'col'), may hold values from -6 to 6
- center: bfloat16 [256, 32768], P('row', 'col'), may hold values from -5 to 5
- radius: bfloat16 [256, 32768], P('row', 'col'), may hold values from 0.049804688 to 1
- lower_gap: bfloat16 [3, 256, 32768], P(None, 'row', 'col'), may hold values from 0.19921875 to 3
- upper_gap: bfloat16 [3, 256, 32768], P(None, 'row', 'col'), may hold values from 0.19921875 to 3
- kernels: float32 [4, 3, 3, 64, 64], replicated, may hold values from -0.25 to 0.25
- biases: float32 [4, 64], replicated, may hold values from -3 to 3
- step_sizes: float32 [3], replicated, may hold values from 0.2 to 1
Outputs:
- bounds: float32 [3], replicated
- final_duals: float32 [3, 256, 32768], P(None, 'row', 'col')
- final_multipliers: float32 [3, 256, 32768], P(None, 'row', 'col')
All inputs are finite; a program needn't handle non-finite values.
Results may differ from a plain program's by a relative error of at most 0.0003.
Values sent between devices are 32-bit elements; how exact they have to be, the bound alone decides.
A program may use at most 128 MiB of HBM per device.

v0:
```python
import jax
import jax.numpy as jnp
from jax import lax
from jax.sharding import PartitionSpec as P

CH = 64
LAYERS = 4
ITERS = 3
TEMP = 0.5
EPS = 1e-06


def extended(cells, sides, width):
    for axis, dim in sides:
        count = lax.axis_size(axis)
        ends = count - 1
        head = lax.slice_in_dim(cells, 0, width, axis=dim)
        tail = lax.slice_in_dim(cells, cells.shape[dim] - width, cells.shape[dim], axis=dim)
        cells = jnp.concatenate(
            [
                lax.ppermute(tail, axis, [(i, (i + 1) % count) for i in range(ends)]),
                cells,
                lax.ppermute(head, axis, [((i + 1) % count, i) for i in range(ends)]),
            ],
            axis=dim,
        )
    return cells


def soft_value(coef, low, high):
    return coef * low - TEMP * jax.nn.softplus(coef * (low - high) / TEMP)


def soft_point(coef, low, high):
    return low + (high - low) * jax.nn.sigmoid(coef * (low - high) / TEMP)


def flipped(kernel):
    return jnp.transpose(kernel[::-1, ::-1], (0, 1, 3, 2))


def conv_valid(padded, kernel):
    out_rows = padded.shape[0] - 2
    out_cols = padded.shape[1] - 2
    in_chan = padded.shape[2]
    result = jnp.zeros((out_rows * out_cols, kernel.shape[3]), jnp.float32)
    for offset_row in range(3):
        for offset_col in range(3):
            window = padded[
                offset_row : offset_row + out_rows, offset_col : offset_col + out_cols
            ].reshape(out_rows * out_cols, in_chan)
            result = result + jnp.dot(
                window,
                kernel[offset_row, offset_col],
                precision=lax.Precision.HIGHEST,
                preferred_element_type=jnp.float32,
            )
    return result.reshape(out_rows, out_cols, kernel.shape[3])


def shards(objective, center, radius, lower_gap, upper_gap, kernels, biases, step_sizes):
    depth = LAYERS - 1
    tile_rows = objective.shape[0]
    tile_cols = objective.shape[1] // CH

    def cube(plane):
        return plane.reshape(plane.shape[:-1] + (tile_cols, CH))

    target = cube(objective)
    target_rim = extended(target, (("row", 0), ("col", 1)), 1)
    target_back = conv_valid(target_rim, flipped(kernels[LAYERS - 1]))
    fixed_part = jnp.sum(target * biases[LAYERS - 1])
    middle = cube(center.astype(jnp.float32))
    half = cube(radius.astype(jnp.float32))
    below = cube(lower_gap.astype(jnp.float32))
    above = cube(upper_gap.astype(jnp.float32))
    zero_map = jnp.zeros_like(middle)
    lows = [middle - half] + [zero_map] * depth
    highs = [middle + half] + [above[j] for j in range(depth)]
    duals = jnp.zeros((depth, tile_rows, tile_cols, CH), jnp.float32)
    multipliers = jnp.zeros_like(duals)
    total_cells = tile_rows * tile_cols * CH * lax.axis_size("row") * lax.axis_size("col")
    bounds = []
    for step in range(ITERS):
        coefs = []
        dual_rim = extended(duals, (("row", 1), ("col", 2)), 1)
        for layer in range(depth):
            coef = -conv_valid(dual_rim[layer], flipped(kernels[layer]))
            if layer > 0:
                coef = coef + multipliers[layer - 1]
            coefs.append(coef)
        points = [soft_point(coefs[layer], lows[layer], highs[layer]) for layer in range(depth)]
        primal = extended(jnp.stack(points), (("row", 1), ("col", 2)), 1)
        input_rims = [primal[layer] for layer in range(depth)]
        coefs.append(target_back + multipliers[depth - 1])
        points.append(soft_point(coefs[depth], lows[depth], highs[depth]))
        value = fixed_part
        for layer in range(LAYERS):
            value = value + jnp.sum(soft_value(coefs[layer], lows[layer], highs[layer]))
        slope_duals = []
        slope_mults = []
        squares = jnp.zeros((), jnp.float32)
        for j in range(depth):
            pos_coef = duals[j] - multipliers[j]
            neg_coef = -duals[j]
            value = value + jnp.sum(soft_value(pos_coef, zero_map, above[j]))
            value = value + jnp.sum(soft_value(neg_coef, zero_map, below[j]))
            value = value - jnp.sum(duals[j] * biases[j])
            positive = soft_point(pos_coef, zero_map, above[j])
            negative = soft_point(neg_coef, zero_map, below[j])
            slope_dual = positive - negative - conv_valid(input_rims[j], kernels[j]) - biases[j]
            slope_mult = points[j + 1] - positive
            squares = squares + jnp.sum(slope_dual * slope_dual) + jnp.sum(slope_mult * slope_mult)
            slope_duals.append(slope_dual)
            slope_mults.append(slope_mult)
        total_squares, total_value = lax.psum((squares, value), ("row", "col"))
        bounds.append(total_value / total_cells)
        scale = step_sizes[step] / jnp.sqrt(total_squares / (2 * depth * total_cells) + EPS)
        duals = duals + scale * jnp.stack(slope_duals)
        multipliers = multipliers + scale * jnp.stack(slope_mults)
    bound_array = jnp.stack(bounds)
    final_duals = duals.reshape(depth, tile_rows, tile_cols * CH)
    final_multipliers = multipliers.reshape(depth, tile_rows, tile_cols * CH)
    return (bound_array, final_duals, final_multipliers)


def solution(mesh):
    placed = (
        P("row", "col"),
        P("row", "col"),
        P("row", "col"),
        P(None, "row", "col"),
        P(None, "row", "col"),
        P(),
        P(),
        P(),
    )
    return jax.shard_map(
        shards,
        mesh=mesh,
        in_specs=placed,
        out_specs=(P(), P(None, "row", "col"), P(None, "row", "col")),
        check_vma=False,
    )
```

profile of v0, /device:TPU:1, one launch (start us, length us, event | category | flops | bytes accessed | tf_op | source)
XLA Modules:
  0.0 666.6 jit_solution(15798143236063260089)
XLA Ops:
  1.3 5.0 collective-permute-start
  8.5 4.0 collective-permute-start.4
  40.0 4.5 collective-permute-start.6
  44.5 1.9 collective-permute-start.7
  54.1 2.1 collective-permute-start.2
  56.2 2.7 collective-permute-start.3
  60.1 2.0 collective-permute-done.3
  82.6 1.8 fusion.139
  86.0 4.3 collective-permute-start.8
  93.7 1.8 neg.745
  96.6 3.1 collective-permute-start.10
  99.8 2.1 collective-permute-start.11
  101.9 2.3 multiply_reduce_fusion.14
  126.6 2.6 subtract_subtract_fusion.11
  133.0 88.6 %psum.43 = f32[]{:T(128)} all-reduce(f32[]{:T(128)S(6)} %add.1337), channel_id=1, replica_groups=mesh['row'=16,'col'=16] {'row','col'}, use_global_device_ids=true, to_apply=%region_21.22 | all-reduce | flops 1 | bytes 8 | tf_op jit(solution)/shard_map/psum | solution.py:116
  224.9 2.1 collective-permute-start.12
  230.0 1.9 collective-permute-done.13
  231.9 3.5 collective-permute-start.14
  235.4 2.3 collective-permute-start.15
  237.9 2.7 collective-permute-done.15
  260.7 2.4 fusion.140
  263.8 2.3 collective-permute-start.16
  268.6 2.6 collective-permute-done.17
  272.7 3.3 collective-permute-start.18
  276.0 2.3 collective-permute-start.19
  309.4 2.7 multiply_subtract_fusion.1
  325.7 2.3 multiply_reduce_fusion.6
  338.0 83.4 %psum.45 = f32[]{:T(128)} all-reduce(f32[]{:T(128)S(6)} %add.1442), channel_id=1, replica_groups=mesh['row'=16,'col'=16] {'row','col'}, use_global_device_ids=true, to_apply=%region_42.43 | all-reduce | flops 1 | bytes 8 | tf_op jit(solution)/shard_map/psum | solution.py:116
  425.9 2.2 collective-permute-start.20
  433.8 1.8 sub.1036
  443.2 3.1 collective-permute-start.22
  446.3 1.9 collective-permute-start.23
  449.4 2.1 collective-permute-done.23
  457.1 2.0 fusion.77
  460.8 2.0 multiply_add_fusion
  475.7 2.5 fusion.142
  479.0 4.9 collective-permute-start.24
  485.4 2.1 fusion.69
  488.2 1.8 stack.110
  493.4 1.8 pad_maximum_fusion.23
  495.3 2.2 collective-permute-start.26
  497.5 2.9 collective-permute-start.27
  500.4 4.4 fusion.41
  504.8 1.8 neg.841
  510.0 1.8 squeeze.655
  538.0 2.5 multiply_subtract_fusion
  551.3 2.2 multiply_reduce_fusion
  578.4 81.8 %all-reduce = (f32[]{:T(128)}, f32[]{:T(128)}, f32[]{:T(128)}, f32[]{:T(128)}) all-reduce(f32[]{:T(128)S(6)} %sub.1093, f32[]{:T(128)S(6)} %sub.1044, f32[]{:T(128)S(6)} %sub.986, f32[]{:T(128)S(6)} %add.1554), channel_id=1, replica_groups=mesh['row'=16,'col'=16] {'row','col'}, use_global_device_ids=true, to_apply=%region_56.57 | all-reduce | flops 4 | bytes 32 | tf_op jit(solution)/shard_map/psum | solution.py:116
  (765 shorter events, 248.4 us)
Async XLA Ops:
  1.3 51.9 %collective-permute-start = (f32[3,1,32,64]{3,2,1,0:T(8,128)}, f32[3,1,32,64]{3,2,1,0:T(8,128)}, u32[]{:S(2)}, u32[]{:S(2)}) collective-permute-start(f32[3,1,32,64]{3,2,1,0:T(8,128)} %broadcast.870), channel_id=1, source_target_pairs={{0,16},{16,32},{32,48},{48,64},{64,80},{80,96},{96,112},{112,128},... | collective-permute-start | bytes 73736 | tf_op jit(solution)/shard_map/ppermute | solution.py:21
  6.2 47.0 %collective-permute-start.1 = (f32[3,1,32,64]{3,2,1,0:T(8,128)}, f32[3,1,32,64]{3,2,1,0:T(8,128)}, u32[]{:S(2)}, u32[]{:S(2)}) collective-permute-start(f32[3,1,32,64]{3,2,1,0:T(8,128)} %broadcast.870), channel_id=1, source_target_pairs={{16,0},{32,16},{48,32},{64,48},{80,64},{96,80},{112,96},{128,112},... | collective-permute-start | bytes 73736 | tf_op jit(solution)/shard_map/ppermute | solution.py:23
  8.5 30.2 %collective-permute-start.4 = (f32[1,32,64]{2,1,0:T(8,128)S(1)}, f32[1,32,64]{2,1,0:T(8,128)S(1)}, u32[]{:S(2)}, u32[]{:S(2)}) collective-permute-start(f32[1,32,64]{2,1,0:T(8,128)S(1)} %slice.1193), channel_id=1, source_target_pairs={{0,16},{16,32},{32,48},{48,64},{64,80},{80,96},{96,112},{112,128},... | collective-permute-start | bytes 24584 | tf_op jit(solution)/shard_map/ppermute | solution.py:21
  13.2 25.5 %collective-permute-start.5 = (f32[1,32,64]{2,1,0:T(8,128)}, f32[1,32,64]{2,1,0:T(8,128)S(1)}, u32[]{:S(2)}, u32[]{:S(2)}) collective-permute-start(f32[1,32,64]{2,1,0:T(8,128)} %slice.1195), channel_id=1, source_target_pairs={{16,0},{32,16},{48,32},{64,48},{80,64},{96,80},{112,96},{128,112},... | collective-permute-start | bytes 24584 | tf_op jit(solution)/shard_map/ppermute | solution.py:23
  15.9 94.7 %copy-start.7 = (f32[3,3,64,64]{3,2,1,0:T(8,128)}, f32[3,3,64,64]{3,2,1,0:T(8,128)S(1)}, u32[]{:S(2)}) copy-start(f32[3,3,64,64]{3,2,1,0:T(8,128)S(1)} %get-tuple-element.93) | copy-start | bytes 442372
  15.9 101.9 %copy-start.10 = (f32[3,3,64,64]{3,2,1,0:T(8,128)}, f32[3,3,64,64]{3,2,1,0:T(8,128)S(1)}, u32[]{:S(2)}) copy-start(f32[3,3,64,64]{3,2,1,0:T(8,128)S(1)} %get-tuple-element.92) | copy-start | bytes 442372
  16.0 107.6 %copy-start.4 = (f32[3,3,64,64]{3,2,1,0:T(8,128)}, f32[3,3,64,64]{3,2,1,0:T(8,128)S(1)}, u32[]{:S(2)}) copy-start(f32[3,3,64,64]{3,2,1,0:T(8,128)S(1)} %get-tuple-element.94) | copy-start | bytes 442372
  18.8 204.2 %copy-start.180 = (f32[64]{0:T(128)}, f32[64]{0:T(128)S(1)}, u32[]{:S(2)}) copy-start(f32[64]{0:T(128)S(1)} %get-tuple-element.365) | copy-start | bytes 772
  18.8 205.3 %copy-start.178 = (f32[64]{0:T(128)}, f32[64]{0:T(128)S(1)}, u32[]{:S(2)}) copy-start(f32[64]{0:T(128)S(1)} %get-tuple-element.367) | copy-start | bytes 772
  18.8 205.3 %copy-start.182 = (f32[64]{0:T(128)}, f32[64]{0:T(128)S(1)}, u32[]{:S(2)}) copy-start(f32[64]{0:T(128)S(1)} %get-tuple-element.368) | copy-start | bytes 772
  28.0 196.2 %copy-start.29 = (f32[1,16,32,64]{3,2,1,0:T(8,128)}, f32[1,16,32,64]{3,2,1,0:T(8,128)S(1)}, u32[]{:S(2)}) copy-start(f32[1,16,32,64]{3,2,1,0:T(8,128)S(1)} %squeeze.619) | copy-start | bytes 393220
  40.0 8.0 %collective-permute-start.6 = (f32[18,1,64]{2,1,0:T(1,128)S(1)}, f32[18,1,64]{2,1,0:T(1,128)S(1)}, u32[]{:S(2)}, u32[]{:S(2)}) collective-permute-start(f32[18,1,64]{2,1,0:T(1,128)S(1)} %get-tuple-element.347), channel_id=1, source_target_pairs={{0,1},{1,2},{2,3},{3,4},{4,5},{5,6},{6,7},{7,8},{8,9},{9,10},{10,1... | collective-permute-start | bytes 13832 | tf_op jit(solution)/shard_map/ppermute | solution.py:21
  44.5 5.0 collective-permute-start.7
  54.1 6.0 collective-permute-start.2
  56.2 5.8 collective-permute-start.3
  86.0 9.5 %collective-permute-start.8 = (f32[3,1,32,64]{3,2,1,0:T(8,128)}, f32[3,1,32,64]{3,2,1,0:T(8,128)S(1)}, u32[]{:S(2)}, u32[]{:S(2)}) collective-permute-start(f32[3,1,32,64]{3,2,1,0:T(8,128)} %get-tuple-element.160), channel_id=1, source_target_pairs={{0,16},{16,32},{32,48},{48,64},{64,80},{80,96},{96,112},{112,128},... | collective-permute-start | bytes 73736 | tf_op jit(solution)/shard_map/ppermute | solution.py:21
  90.3 5.7 collective-permute-start.9
  96.6 9.3 %collective-permute-start.10 = (f32[3,18,1,64]{3,2,1,0:T(1,128)}, f32[3,18,1,64]{3,2,1,0:T(1,128)S(1)}, u32[]{:S(2)}, u32[]{:S(2)}) collective-permute-start(f32[3,18,1,64]{3,2,1,0:T(1,128)} %get-tuple-element.121), channel_id=1, source_target_pairs={{0,1},{1,2},{2,3},{3,4},{4,5},{5,6},{6,7},{7,8},{8,9},{9,10},{10,1... | collective-permute-start | bytes 41480 | tf_op jit(solution)/shard_map/ppermute | solution.py:21
  99.8 6.1 collective-permute-start.11
  126.6 96.4 %copy-start.39 = (f32[1,16,32,64]{3,2,1,0:T(8,128)S(1)}, f32[1,16,32,64]{3,2,1,0:T(8,128)}, u32[]{:S(2)}) copy-start(f32[1,16,32,64]{3,2,1,0:T(8,128)} %squeeze.618) | copy-start | bytes 393220
  129.2 95.0 %copy-start.34 = (f32[1,16,32,64]{3,2,1,0:T(8,128)S(1)}, f32[1,16,32,64]{3,2,1,0:T(8,128)}, u32[]{:S(2)}) copy-start(f32[1,16,32,64]{3,2,1,0:T(8,128)} %squeeze.620) | copy-start | bytes 393220
  133.0 91.5 %copy-start.37 = (f32[1,16,32,64]{3,2,1,0:T(8,128)}, f32[1,16,32,64]{3,2,1,0:T(8,128)S(1)}, u32[]{:S(2)}) copy-start(f32[1,16,32,64]{3,2,1,0:T(8,128)S(1)} %squeeze.621) | copy-start | bytes 393220
  224.9 5.0 collective-permute-start.12
  227.0 4.8 collective-permute-start.13
  231.9 5.9 collective-permute-start.14
  235.4 5.2 collective-permute-start.15
  263.8 4.8 collective-permute-start.16
  266.1 5.2 collective-permute-start.17
  272.7 22.6 %collective-permute-start.18 = (f32[3,18,1,64]{3,2,1,0:T(1,128)}, f32[3,18,1,64]{3,2,1,0:T(1,128)}, u32[]{:S(2)}, u32[]{:S(2)}) collective-permute-start(f32[3,18,1,64]{3,2,1,0:T(1,128)} %get-tuple-element.117), channel_id=1, source_target_pairs={{0,1},{1,2},{2,3},{3,4},{4,5},{5,6},{6,7},{7,8},{8,9},{9,10},{10,1... | collective-permute-start | bytes 41480 | tf_op jit(solution)/shard_map/ppermute | solution.py:21
  276.0 19.3 %collective-permute-start.19 = (f32[3,18,1,64]{3,2,1,0:T(1,128)}, f32[3,18,1,64]{3,2,1,0:T(1,128)}, u32[]{:S(2)}, u32[]{:S(2)}) collective-permute-start(f32[3,18,1,64]{3,2,1,0:T(1,128)} %get-tuple-element.118), channel_id=1, source_target_pairs={{1,0},{2,1},{3,2},{4,3},{5,4},{6,5},{7,6},{8,7},{9,8},{10,9},{11,1... | collective-permute-start | bytes 41480 | tf_op jit(solution)/shard_map/ppermute | solution.py:23
  425.9 16.4 %collective-permute-start.20 = (f32[3,1,32,64]{3,2,1,0:T(8,128)}, f32[3,1,32,64]{3,2,1,0:T(8,128)}, u32[]{:S(2)}, u32[]{:S(2)}) collective-permute-start(f32[3,1,32,64]{3,2,1,0:T(8,128)} %get-tuple-element.150), channel_id=1, source_target_pairs={{0,16},{16,32},{32,48},{48,64},{64,80},{80,96},{96,112},{112,128},... | collective-permute-start | bytes 73736 | tf_op jit(solution)/shard_map/ppermute | solution.py:21
  428.1 14.2 %collective-permute-start.21 = (f32[3,1,32,64]{3,2,1,0:T(8,128)}, f32[3,1,32,64]{3,2,1,0:T(8,128)}, u32[]{:S(2)}, u32[]{:S(2)}) collective-permute-start(f32[3,1,32,64]{3,2,1,0:T(8,128)} %get-tuple-element.151), channel_id=1, source_target_pairs={{16,0},{32,16},{48,32},{64,48},{80,64},{96,80},{112,96},{128,112},... | collective-permute-start | bytes 73736 | tf_op jit(solution)/shard_map/ppermute | solution.py:23
  443.2 6.2 collective-permute-start.22
  446.3 5.2 collective-permute-start.23
  479.0 14.4 %collective-permute-start.24 = (f32[3,1,32,64]{3,2,1,0:T(8,128)}, f32[3,1,32,64]{3,2,1,0:T(8,128)}, u32[]{:S(2)}, u32[]{:S(2)}) collective-permute-start(f32[3,1,32,64]{3,2,1,0:T(8,128)} %get-tuple-element.143), channel_id=1, source_target_pairs={{0,16},{16,32},{32,48},{48,64},{64,80},{80,96},{96,112},{112,128},... | collective-permute-start | bytes 73736 | tf_op jit(solution)/shard_map/ppermute | solution.py:21
  483.9 9.5 %collective-permute-start.25 = (f32[3,1,32,64]{3,2,1,0:T(8,128)}, f32[3,1,32,64]{3,2,1,0:T(8,128)}, u32[]{:S(2)}, u32[]{:S(2)}) collective-permute-start(f32[3,1,32,64]{3,2,1,0:T(8,128)} %get-tuple-element.144), channel_id=1, source_target_pairs={{16,0},{32,16},{48,32},{64,48},{80,64},{96,80},{112,96},{128,112},... | collective-permute-start | bytes 73736 | tf_op jit(solution)/shard_map/ppermute | solution.py:23
  495.3 27.7 %collective-permute-start.26 = (f32[3,18,1,64]{3,2,1,0:T(1,128)}, f32[3,18,1,64]{3,2,1,0:T(1,128)}, u32[]{:S(2)}, u32[]{:S(2)}) collective-permute-start(f32[3,18,1,64]{3,2,1,0:T(1,128)} %get-tuple-element.113), channel_id=1, source_target_pairs={{0,1},{1,2},{2,3},{3,4},{4,5},{5,6},{6,7},{7,8},{8,9},{9,10},{10,1... | collective-permute-start | bytes 41480 | tf_op jit(solution)/shard_map/ppermute | solution.py:21
  497.5 25.5 %collective-permute-start.27 = (f32[3,18,1,64]{3,2,1,0:T(1,128)}, f32[3,18,1,64]{3,2,1,0:T(1,128)}, u32[]{:S(2)}, u32[]{:S(2)}) collective-permute-start(f32[3,18,1,64]{3,2,1,0:T(1,128)} %get-tuple-element.114), channel_id=1, source_target_pairs={{1,0},{2,1},{3,2},{4,3},{5,4},{6,5},{7,6},{8,7},{9,8},{10,9},{11,1... | collective-permute-start | bytes 41480 | tf_op jit(solution)/shard_map/ppermute | solution.py:23
  553.5 107.4 %copy-start.126 = (f32[1,16,32,64]{3,2,1,0:T(8,128)S(1)}, f32[1,16,32,64]{3,2,1,0:T(8,128)}, u32[]{:S(2)}) copy-start(f32[1,16,32,64]{3,2,1,0:T(8,128)} %get-tuple-element.81) | copy-start | bytes 393220
  556.1 105.1 %copy-start.125 = (f32[1,16,32,64]{3,2,1,0:T(8,128)S(1)}, f32[1,16,32,64]{3,2,1,0:T(8,128)}, u32[]{:S(2)}) copy-start(f32[1,16,32,64]{3,2,1,0:T(8,128)} %get-tuple-element.127) | copy-start | bytes 393220
  556.1 105.3 %copy-start.124 = (f32[1,16,32,64]{3,2,1,0:T(8,128)S(1)}, f32[1,16,32,64]{3,2,1,0:T(8,128)}, u32[]{:S(2)}) copy-start(f32[1,16,32,64]{3,2,1,0:T(8,128)} %get-tuple-element.82) | copy-start | bytes 393220
  557.1 107.6 %copy-start.135 = (f32[1,16,2048]{2,1,0:T(8,128)S(1)}, f32[1,16,2048]{2,1,0:T(8,128)}, u32[]{:S(2)}) copy-start(f32[1,16,2048]{2,1,0:T(8,128)} %get-tuple-element.170) | copy-start | bytes 393220
  557.1 107.6 %copy-start.136 = (f32[1,16,2048]{2,1,0:T(8,128)S(1)}, f32[1,16,2048]{2,1,0:T(8,128)}, u32[]{:S(2)}) copy-start(f32[1,16,2048]{2,1,0:T(8,128)} %get-tuple-element.172) | copy-start | bytes 393220
  557.1 107.6 %copy-start.139 = (f32[1,16,2048]{2,1,0:T(8,128)S(1)}, f32[1,16,2048]{2,1,0:T(8,128)}, u32[]{:S(2)}) copy-start(f32[1,16,2048]{2,1,0:T(8,128)} %stack.119) | copy-start | bytes 393220
  557.1 107.6 %copy-start.140 = (f32[1,16,2048]{2,1,0:T(8,128)S(1)}, f32[1,16,2048]{2,1,0:T(8,128)}, u32[]{:S(2)}) copy-start(f32[1,16,2048]{2,1,0:T(8,128)} %stack.120) | copy-start | bytes 393220
  557.1 107.6 %copy-start.147 = (f32[1,16,2048]{2,1,0:T(8,128)S(1)}, f32[1,16,2048]{2,1,0:T(8,128)}, u32[]{:S(2)}) copy-start(f32[1,16,2048]{2,1,0:T(8,128)} %stack.121) | copy-start | bytes 393220
  557.1 107.6 %copy-start.148 = (f32[1,16,2048]{2,1,0:T(8,128)S(1)}, f32[1,16,2048]{2,1,0:T(8,128)}, u32[]{:S(2)}) copy-start(f32[1,16,2048]{2,1,0:T(8,128)} %stack.123) | copy-start | bytes 393220
  557.1 107.6 %copy-start.153 = (f32[1,16,2048]{2,1,0:T(8,128)S(1)}, f32[1,16,2048]{2,1,0:T(8,128)}, u32[]{:S(2)}) copy-start(f32[1,16,2048]{2,1,0:T(8,128)} %get-tuple-element.75) | copy-start | bytes 393220
  (170 other events, 1273.9 us)
where the time goes:
time: 675 us; the launch traced here: 667 us
  blocking collectives  254 us (38%)
  local copies, waits for them, and re-layouts  125 us (19%)
  matrix products  87.9 us (13%)
  starting transfers between devices  72.2 us (11%)
  other arithmetic  66.3 us (10%)
  between operations  47.9 us (7%)
  waiting for transfers between devices  13.4 us (2%)
    psum x3, blocking collectives, shards(): total_squares, total_value = lax.psum((squares, value), ('row', 'col'))  254 us
    dot_general x171, matrix products, conv_valid(): jnp.dot(window, kernel[offset_row, offset_col], precision=lax.Precision.H...  87.9 us
    ppermute x14, starting transfers between devices, extended(): lax.ppermute(tail, axis, [(i, (i + 1) % count) for i in range(ends)])  46.5 us
    ppermute x14, starting transfers between devices, extended(): lax.ppermute(head, axis, [((i + 1) % count, i) for i in range(ends)])  25.6 us
    neg x15, local copies, waits for them, and re-layouts, shards(): coef = -conv_valid(dual_rim[layer], flipped(kernels[layer]))  21.6 us
  transfers between devices with their start and end apart: 28, of which 7 were waited for; matrix products, arithmetic and copies ran while one was open for 15% of the time, Pallas kernels for 0%

commit v1 on v0

--- a/solution.py
+++ b/solution.py
@@ -113,7 +113,7 @@
             squares = squares + jnp.sum(slope_dual * slope_dual) + jnp.sum(slope_mult * slope_mult)
             slope_duals.append(slope_dual)
             slope_mults.append(slope_mult)
-        total_squares, total_value = lax.psum((squares, value), ("row", "col"))
+        total_squares, total_value = lax.psum(lax.psum((squares, value), "col"), "row")
         bounds.append(total_value / total_cells)
         scale = step_sizes[step] / jnp.sqrt(total_squares / (2 * depth * total_cells) + EPS)
         duals = duals + scale * jnp.stack(slope_duals)

time: 675 us -> 643 us (0.953)
  the two profiles are of different devices: /device:TPU:1 before, /device:TPU:4 now
where the time goes in v1:
time: 643 us; the launch traced here: 634 us
  blocking collectives  211 us (33%)
  local copies, waits for them, and re-layouts  122 us (19%)
  starting transfers between devices  95.4 us (15%)
  matrix products  87.1 us (14%)
  other arithmetic  63.8 us (10%)
  between operations  47.6 us (7%)
  waiting for transfers between devices  6.76 us (1%)
    psum x3, blocking collectives, shards(): lax.psum(lax.psum((squares, value), 'col'), 'row')  121 us
    psum x3, blocking collectives, shards(): lax.psum((squares, value), 'col')  90.1 us
    dot_general x171, matrix products, conv_valid(): jnp.dot(window, kernel[offset_row, offset_col], precision=lax.Precision.H...  87.1 us
    ppermute x14, starting transfers between devices, extended(): lax.ppermute(head, axis, [((i + 1) % count, i) for i in range(ends)])  62.3 us
    ppermute x14, starting transfers between devices, extended(): lax.ppermute(tail, axis, [(i, (i + 1) % count) for i in range(ends)])  33.1 us
    neg x15, local copies, waits for them, and re-layouts, shards(): coef = -conv_valid(dual_rim[layer], flipped(kernels[layer]))  20.7 us
    sub x7, other arithmetic, shards(): slope_mult = points[j + 1] - positive  13 us
  transfers between devices with their start and end apart: 28, of which 7 were waited for; matrix products, arithmetic and copies ran while one was open for 15% of the time, Pallas kernels for 0%

profile of v1, /device:TPU:4, one launch (start us, length us, event | category | flops | bytes accessed | tf_op | source)
XLA Modules:
  0.0 634.3 jit_solution(4564089453791105754)
XLA Ops:
  1.3 3.8 collective-permute-start
  5.1 5.8 collective-permute-start.1
  11.9 1.9 collective-permute-start.4
  14.5 7.7 %collective-permute-start.5 = (f32[1,32,64]{2,1,0:T(8,128)}, f32[1,32,64]{2,1,0:T(8,128)S(1)}, u32[]{:S(2)}, u32[]{:S(2)}) collective-permute-start(f32[1,32,64]{2,1,0:T(8,128)} %slice.1195), channel_id=1, source_target_pairs={{16,0},{32,16},{48,32},{64,48},{80,64},{96,80},{112,96},{128,112},... | collective-permute-start | bytes 24584 | tf_op jit(solution)/shard_map/ppermute | solution.py:23
  36.5 1.8 copy.172
  49.0 2.6 collective-permute-done.7
  56.1 4.3 collective-permute-start.2
  60.5 1.8 collective-permute-start.3
  82.6 1.8 fusion.139
  86.0 1.9 collective-permute-start.8
  87.9 7.5 %collective-permute-start.9 = (f32[3,1,32,64]{3,2,1,0:T(8,128)}, f32[3,1,32,64]{3,2,1,0:T(8,128)S(1)}, u32[]{:S(2)}, u32[]{:S(2)}) collective-permute-start(f32[3,1,32,64]{3,2,1,0:T(8,128)} %get-tuple-element.165), channel_id=1, source_target_pairs={{16,0},{32,16},{48,32},{64,48},{80,64},{96,80},{112,96},{128,112},... | collective-permute-start | bytes 73736 | tf_op jit(solution)/shard_map/ppermute | solution.py:23
  99.4 3.6 collective-permute-start.10
  104.5 2.3 multiply_reduce_fusion.14
  127.6 2.7 subtract_subtract_fusion.11
  134.1 32.0 %psum.86 = f32[]{:T(128)} all-reduce(f32[]{:T(128)S(6)} %add.1349), channel_id=1, replica_groups=mesh['row'=16,'col'=16] {'col'}, use_global_device_ids=true, to_apply=%region_22.23 | all-reduce | flops 1 | bytes 8 | tf_op jit(solution)/shard_map/psum | solution.py:116
  167.1 41.4 %psum.87 = f32[]{:T(128)} all-reduce(f32[]{:T(128)} %psum.86), channel_id=1, replica_groups=mesh['row'=16,'col'=16] {'row'}, use_global_device_ids=true, to_apply=%region_23.24 | all-reduce | flops 1 | bytes 8 | tf_op jit(solution)/shard_map/psum | solution.py:116
  211.8 2.1 collective-permute-start.12
  213.9 7.5 %collective-permute-start.13 = (f32[3,1,32,64]{3,2,1,0:T(8,128)S(1)}, f32[3,1,32,64]{3,2,1,0:T(8,128)S(1)}, u32[]{:S(2)}, u32[]{:S(2)}) collective-permute-start(f32[3,1,32,64]{3,2,1,0:T(8,128)S(1)} %get-tuple-element.163), channel_id=1, source_target_pairs={{16,0},{32,16},{48,32},{64,48},{80,64},{96,80},{112,96},{128,112},... | collective-permute-start | bytes 73736 | tf_op jit(solution)/shard_map/ppermute | solution.py:23
  247.8 2.4 fusion.140
  250.2 2.1 collective-permute-start.16
  252.2 7.9 %collective-permute-start.17 = (f32[3,1,32,64]{3,2,1,0:T(8,128)S(1)}, f32[3,1,32,64]{3,2,1,0:T(8,128)S(1)}, u32[]{:S(2)}, u32[]{:S(2)}) collective-permute-start(f32[3,1,32,64]{3,2,1,0:T(8,128)S(1)} %get-tuple-element.161), channel_id=1, source_target_pairs={{16,0},{32,16},{48,32},{64,48},{80,64},{96,80},{112,96},{128,112},... | collective-permute-start | bytes 73736 | tf_op jit(solution)/shard_map/ppermute | solution.py:23
  263.0 2.7 collective-permute-start.18
  298.1 2.6 multiply_subtract_fusion.1
  300.7 1.8 squeeze.642
  314.3 2.3 multiply_reduce_fusion.6
  327.0 29.2 %psum.90 = f32[]{:T(128)} all-reduce(f32[]{:T(128)S(6)} %add.1454), channel_id=1, replica_groups=mesh['row'=16,'col'=16] {'col'}, use_global_device_ids=true, to_apply=%region_45.46 | all-reduce | flops 1 | bytes 8 | tf_op jit(solution)/shard_map/psum | solution.py:116
  356.9 42.1 %psum.91 = f32[]{:T(128)} all-reduce(f32[]{:T(128)} %psum.90), channel_id=1, replica_groups=mesh['row'=16,'col'=16] {'row'}, use_global_device_ids=true, to_apply=%region_46.47 | all-reduce | flops 1 | bytes 8 | tf_op jit(solution)/shard_map/psum | solution.py:116
  404.5 1.9 collective-permute-start.20
  406.4 7.7 %collective-permute-start.21 = (f32[3,1,32,64]{3,2,1,0:T(8,128)}, f32[3,1,32,64]{3,2,1,0:T(8,128)}, u32[]{:S(2)}, u32[]{:S(2)}) collective-permute-start(f32[3,1,32,64]{3,2,1,0:T(8,128)} %get-tuple-element.155), channel_id=1, source_target_pairs={{16,0},{32,16},{48,32},{64,48},{80,64},{96,80},{112,96},{128,112},... | collective-permute-start | bytes 73736 | tf_op jit(solution)/shard_map/ppermute | solution.py:23
  416.6 1.8 sub.1031
  418.4 1.8 sub.1036
  437.7 2.0 fusion.77
  441.4 2.0 multiply_add_fusion
  456.4 2.5 fusion.142
  459.7 1.9 collective-permute-start.24
  461.6 7.7 %collective-permute-start.25 = (f32[3,1,32,64]{3,2,1,0:T(8,128)}, f32[3,1,32,64]{3,2,1,0:T(8,128)}, u32[]{:S(2)}, u32[]{:S(2)}) collective-permute-start(f32[3,1,32,64]{3,2,1,0:T(8,128)} %get-tuple-element.148), channel_id=1, source_target_pairs={{16,0},{32,16},{48,32},{64,48},{80,64},{96,80},{112,96},{128,112},... | collective-permute-start | bytes 73736 | tf_op jit(solution)/shard_map/ppermute | solution.py:23
  469.3 2.1 fusion.69
  472.2 1.8 stack.110
  477.4 1.8 pad_maximum_fusion.23
  479.2 3.0 collective-permute-start.26
  483.7 4.4 fusion.41
  488.1 1.8 neg.841
  491.6 1.8 copy.234
  493.4 1.8 squeeze.655
  521.2 2.5 multiply_subtract_fusion
  534.5 2.2 multiply_reduce_fusion
  561.4 28.9 %all-reduce = (f32[]{:T(128)}, f32[]{:T(128)}, f32[]{:T(128)}, f32[]{:T(128)}) all-reduce(f32[]{:T(128)S(6)} %sub.1093, f32[]{:T(128)S(6)} %sub.1044, f32[]{:T(128)S(6)} %sub.986, f32[]{:T(128)S(6)} %add.1566), channel_id=1, replica_groups=mesh['row'=16,'col'=16] {'col'}, use_global_device_ids=true, to_apply=%region_60.61 | all-reduce | flops 4 | bytes 32 | tf_op jit(solution)/shard_map/psum | solution.py:116
  590.4 37.6 %all-reduce.1 = (f32[]{:T(128)}, f32[]{:T(128)}, f32[]{:T(128)}, f32[]{:T(128)}) all-reduce(f32[]{:T(128)} %get-tuple-element.56, f32[]{:T(128)} %get-tuple-element.57, f32[]{:T(128)} %get-tuple-element.58, f32[]{:T(128)} %get-tuple-element.59), channel_id=1, replica_groups=mesh['row'=16,'col'=16] {'row'}, use_global_device_ids=true, to_apply=%region_61.62 | all-reduce | flops 4 | bytes 32 | tf_op jit(solution)/shard_map/psum | solution.py:116
  (784 shorter events, 242.5 us)
Async XLA Ops:
  1.3 54.0 %collective-permute-start = (f32[3,1,32,64]{3,2,1,0:T(8,128)}, f32[3,1,32,64]{3,2,1,0:T(8,128)}, u32[]{:S(2)}, u32[]{:S(2)}) collective-permute-start(f32[3,1,32,64]{3,2,1,0:T(8,128)} %broadcast.870), channel_id=1, source_target_pairs={{0,16},{16,32},{32,48},{48,64},{64,80},{80,96},{96,112},{112,128},... | collective-permute-start | bytes 73736 | tf_op jit(solution)/shard_map/ppermute | solution.py:21
  5.1 50.2 %collective-permute-start.1 = (f32[3,1,32,64]{3,2,1,0:T(8,128)}, f32[3,1,32,64]{3,2,1,0:T(8,128)}, u32[]{:S(2)}, u32[]{:S(2)}) collective-permute-start(f32[3,1,32,64]{3,2,1,0:T(8,128)} %broadcast.870), channel_id=1, source_target_pairs={{16,0},{32,16},{48,32},{64,48},{80,64},{96,80},{112,96},{128,112},... | collective-permute-start | bytes 73736 | tf_op jit(solution)/shard_map/ppermute | solution.py:23
  11.9 31.6 %collective-permute-start.4 = (f32[1,32,64]{2,1,0:T(8,128)S(1)}, f32[1,32,64]{2,1,0:T(8,128)S(1)}, u32[]{:S(2)}, u32[]{:S(2)}) collective-permute-start(f32[1,32,64]{2,1,0:T(8,128)S(1)} %slice.1193), channel_id=1, source_target_pairs={{0,16},{16,32},{32,48},{48,64},{64,80},{80,96},{96,112},{112,128},... | collective-permute-start | bytes 24584 | tf_op jit(solution)/shard_map/ppermute | solution.py:21
  14.5 29.1 %collective-permute-start.5 = (f32[1,32,64]{2,1,0:T(8,128)}, f32[1,32,64]{2,1,0:T(8,128)S(1)}, u32[]{:S(2)}, u32[]{:S(2)}) collective-permute-start(f32[1,32,64]{2,1,0:T(8,128)} %slice.1195), channel_id=1, source_target_pairs={{16,0},{32,16},{48,32},{64,48},{80,64},{96,80},{112,96},{128,112},... | collective-permute-start | bytes 24584 | tf_op jit(solution)/shard_map/ppermute | solution.py:23
  23.5 89.7 %copy-start.7 = (f32[3,3,64,64]{3,2,1,0:T(8,128)}, f32[3,3,64,64]{3,2,1,0:T(8,128)S(1)}, u32[]{:S(2)}) copy-start(f32[3,3,64,64]{3,2,1,0:T(8,128)S(1)} %get-tuple-element.97) | copy-start | bytes 442372
  23.5 96.9 %copy-start.10 = (f32[3,3,64,64]{3,2,1,0:T(8,128)}, f32[3,3,64,64]{3,2,1,0:T(8,128)S(1)}, u32[]{:S(2)}) copy-start(f32[3,3,64,64]{3,2,1,0:T(8,128)S(1)} %get-tuple-element.96) | copy-start | bytes 442372
  23.5 102.6 %copy-start.4 = (f32[3,3,64,64]{3,2,1,0:T(8,128)}, f32[3,3,64,64]{3,2,1,0:T(8,128)S(1)}, u32[]{:S(2)}) copy-start(f32[3,3,64,64]{3,2,1,0:T(8,128)S(1)} %get-tuple-element.98) | copy-start | bytes 442372
  26.3 183.5 %copy-start.188 = (f32[64]{0:T(128)}, f32[64]{0:T(128)S(1)}, u32[]{:S(2)}) copy-start(f32[64]{0:T(128)S(1)} %get-tuple-element.369) | copy-start | bytes 772
  26.3 184.7 %copy-start.186 = (f32[64]{0:T(128)}, f32[64]{0:T(128)S(1)}, u32[]{:S(2)}) copy-start(f32[64]{0:T(128)S(1)} %get-tuple-element.371) | copy-start | bytes 772
  26.3 184.7 %copy-start.190 = (f32[64]{0:T(128)}, f32[64]{0:T(128)S(1)}, u32[]{:S(2)}) copy-start(f32[64]{0:T(128)S(1)} %get-tuple-element.372) | copy-start | bytes 772
  35.6 175.5 %copy-start.29 = (f32[1,16,32,64]{3,2,1,0:T(8,128)}, f32[1,16,32,64]{3,2,1,0:T(8,128)S(1)}, u32[]{:S(2)}) copy-start(f32[1,16,32,64]{3,2,1,0:T(8,128)S(1)} %squeeze.619) | copy-start | bytes 393220
  44.8 4.1 collective-permute-start.6
  46.1 5.4 collective-permute-start.7
  56.1 7.2 %collective-permute-start.2 = (f32[3,18,1,64]{3,2,1,0:T(1,128)S(1)}, f32[3,18,1,64]{3,2,1,0:T(1,128)S(1)}, u32[]{:S(2)}, u32[]{:S(2)}) collective-permute-start(f32[3,18,1,64]{3,2,1,0:T(1,128)S(1)} %get-tuple-element.127), channel_id=1, source_target_pairs={{0,1},{1,2},{2,3},{3,4},{4,5},{5,6},{6,7},{7,8},{8,9},{9,10},{10,1... | collective-permute-start | bytes 41480 | tf_op jit(solution)/shard_map/ppermute | solution.py:21
  60.5 3.1 collective-permute-start.3
  86.0 12.7 %collective-permute-start.8 = (f32[3,1,32,64]{3,2,1,0:T(8,128)}, f32[3,1,32,64]{3,2,1,0:T(8,128)S(1)}, u32[]{:S(2)}, u32[]{:S(2)}) collective-permute-start(f32[3,1,32,64]{3,2,1,0:T(8,128)} %get-tuple-element.164), channel_id=1, source_target_pairs={{0,16},{16,32},{32,48},{48,64},{64,80},{80,96},{96,112},{112,128},... | collective-permute-start | bytes 73736 | tf_op jit(solution)/shard_map/ppermute | solution.py:21
  87.9 10.8 %collective-permute-start.9 = (f32[3,1,32,64]{3,2,1,0:T(8,128)}, f32[3,1,32,64]{3,2,1,0:T(8,128)S(1)}, u32[]{:S(2)}, u32[]{:S(2)}) collective-permute-start(f32[3,1,32,64]{3,2,1,0:T(8,128)} %get-tuple-element.165), channel_id=1, source_target_pairs={{16,0},{32,16},{48,32},{64,48},{80,64},{96,80},{112,96},{128,112},... | collective-permute-start | bytes 73736 | tf_op jit(solution)/shard_map/ppermute | solution.py:23
  99.4 9.1 %collective-permute-start.10 = (f32[3,18,1,64]{3,2,1,0:T(1,128)}, f32[3,18,1,64]{3,2,1,0:T(1,128)S(1)}, u32[]{:S(2)}, u32[]{:S(2)}) collective-permute-start(f32[3,18,1,64]{3,2,1,0:T(1,128)} %get-tuple-element.125), channel_id=1, source_target_pairs={{0,1},{1,2},{2,3},{3,4},{4,5},{5,6},{6,7},{7,8},{8,9},{9,10},{10,1... | collective-permute-start | bytes 41480 | tf_op jit(solution)/shard_map/ppermute | solution.py:21
  103.0 5.5 collective-permute-start.11
  127.5 82.3 %copy-start.39 = (f32[1,16,32,64]{3,2,1,0:T(8,128)S(1)}, f32[1,16,32,64]{3,2,1,0:T(8,128)}, u32[]{:S(2)}) copy-start(f32[1,16,32,64]{3,2,1,0:T(8,128)} %squeeze.618) | copy-start | bytes 393220
  130.2 80.8 %copy-start.55 = (f32[512,64]{1,0:T(8,128)S(1)}, f32[512,64]{1,0:T(8,128)}, u32[]{:S(2)}) copy-start(f32[512,64]{1,0:T(8,128)} %copy-done.54) | copy-start | bytes 393220
  211.8 9.7 %collective-permute-start.12 = (f32[3,1,32,64]{3,2,1,0:T(8,128)S(1)}, f32[3,1,32,64]{3,2,1,0:T(8,128)S(1)}, u32[]{:S(2)}, u32[]{:S(2)}) collective-permute-start(f32[3,1,32,64]{3,2,1,0:T(8,128)S(1)} %get-tuple-element.162), channel_id=1, source_target_pairs={{0,16},{16,32},{32,48},{48,64},{64,80},{80,96},{96,112},{112,128},... | collective-permute-start | bytes 73736 | tf_op jit(solution)/shard_map/ppermute | solution.py:21
  213.9 9.3 %collective-permute-start.13 = (f32[3,1,32,64]{3,2,1,0:T(8,128)S(1)}, f32[3,1,32,64]{3,2,1,0:T(8,128)S(1)}, u32[]{:S(2)}, u32[]{:S(2)}) collective-permute-start(f32[3,1,32,64]{3,2,1,0:T(8,128)S(1)} %get-tuple-element.163), channel_id=1, source_target_pairs={{16,0},{32,16},{48,32},{64,48},{80,64},{96,80},{112,96},{128,112},... | collective-permute-start | bytes 73736 | tf_op jit(solution)/shard_map/ppermute | solution.py:23
  223.2 2.9 collective-permute-start.14
  224.5 3.1 collective-permute-start.15
  250.2 11.6 %collective-permute-start.16 = (f32[3,1,32,64]{3,2,1,0:T(8,128)S(1)}, f32[3,1,32,64]{3,2,1,0:T(8,128)S(1)}, u32[]{:S(2)}, u32[]{:S(2)}) collective-permute-start(f32[3,1,32,64]{3,2,1,0:T(8,128)S(1)} %get-tuple-element.160), channel_id=1, source_target_pairs={{0,16},{16,32},{32,48},{48,64},{64,80},{80,96},{96,112},{112,128},... | collective-permute-start | bytes 73736 | tf_op jit(solution)/shard_map/ppermute | solution.py:21
  252.2 9.6 %collective-permute-start.17 = (f32[3,1,32,64]{3,2,1,0:T(8,128)S(1)}, f32[3,1,32,64]{3,2,1,0:T(8,128)S(1)}, u32[]{:S(2)}, u32[]{:S(2)}) collective-permute-start(f32[3,1,32,64]{3,2,1,0:T(8,128)S(1)} %get-tuple-element.161), channel_id=1, source_target_pairs={{16,0},{32,16},{48,32},{64,48},{80,64},{96,80},{112,96},{128,112},... | collective-permute-start | bytes 73736 | tf_op jit(solution)/shard_map/ppermute | solution.py:23
  263.0 21.0 %collective-permute-start.18 = (f32[3,18,1,64]{3,2,1,0:T(1,128)}, f32[3,18,1,64]{3,2,1,0:T(1,128)}, u32[]{:S(2)}, u32[]{:S(2)}) collective-permute-start(f32[3,18,1,64]{3,2,1,0:T(1,128)} %get-tuple-element.121), channel_id=1, source_target_pairs={{0,1},{1,2},{2,3},{3,4},{4,5},{5,6},{6,7},{7,8},{8,9},{9,10},{10,1... | collective-permute-start | bytes 41480 | tf_op jit(solution)/shard_map/ppermute | solution.py:21
  265.7 18.4 %collective-permute-start.19 = (f32[3,18,1,64]{3,2,1,0:T(1,128)}, f32[3,18,1,64]{3,2,1,0:T(1,128)}, u32[]{:S(2)}, u32[]{:S(2)}) collective-permute-start(f32[3,18,1,64]{3,2,1,0:T(1,128)} %get-tuple-element.122), channel_id=1, source_target_pairs={{1,0},{2,1},{3,2},{4,3},{5,4},{6,5},{7,6},{8,7},{9,8},{10,9},{11,1... | collective-permute-start | bytes 41480 | tf_op jit(solution)/shard_map/ppermute | solution.py:23
  322.0 78.7 %copy-start.30 = (f32[1,16,32,64]{3,2,1,0:T(8,128)S(1)}, f32[1,16,32,64]{3,2,1,0:T(8,128)}, u32[]{:S(2)}) copy-start(f32[1,16,32,64]{3,2,1,0:T(8,128)} %copy-done.29) | copy-start | bytes 393220
  404.5 22.4 %collective-permute-start.20 = (f32[3,1,32,64]{3,2,1,0:T(8,128)}, f32[3,1,32,64]{3,2,1,0:T(8,128)}, u32[]{:S(2)}, u32[]{:S(2)}) collective-permute-start(f32[3,1,32,64]{3,2,1,0:T(8,128)} %get-tuple-element.154), channel_id=1, source_target_pairs={{0,16},{16,32},{32,48},{48,64},{64,80},{80,96},{96,112},{112,128},... | collective-permute-start | bytes 73736 | tf_op jit(solution)/shard_map/ppermute | solution.py:21
  406.4 20.4 %collective-permute-start.21 = (f32[3,1,32,64]{3,2,1,0:T(8,128)}, f32[3,1,32,64]{3,2,1,0:T(8,128)}, u32[]{:S(2)}, u32[]{:S(2)}) collective-permute-start(f32[3,1,32,64]{3,2,1,0:T(8,128)} %get-tuple-element.155), channel_id=1, source_target_pairs={{16,0},{32,16},{48,32},{64,48},{80,64},{96,80},{112,96},{128,112},... | collective-permute-start | bytes 73736 | tf_op jit(solution)/shard_map/ppermute | solution.py:23
  427.7 3.7 collective-permute-start.22
  429.0 3.1 collective-permute-start.23
  459.7 17.7 %collective-permute-start.24 = (f32[3,1,32,64]{3,2,1,0:T(8,128)}, f32[3,1,32,64]{3,2,1,0:T(8,128)}, u32[]{:S(2)}, u32[]{:S(2)}) collective-permute-start(f32[3,1,32,64]{3,2,1,0:T(8,128)} %get-tuple-element.147), channel_id=1, source_target_pairs={{0,16},{16,32},{32,48},{48,64},{64,80},{80,96},{96,112},{112,128},... | collective-permute-start | bytes 73736 | tf_op jit(solution)/shard_map/ppermute | solution.py:21
  461.6 15.8 %collective-permute-start.25 = (f32[3,1,32,64]{3,2,1,0:T(8,128)}, f32[3,1,32,64]{3,2,1,0:T(8,128)}, u32[]{:S(2)}, u32[]{:S(2)}) collective-permute-start(f32[3,1,32,64]{3,2,1,0:T(8,128)} %get-tuple-element.148), channel_id=1, source_target_pairs={{16,0},{32,16},{48,32},{64,48},{80,64},{96,80},{112,96},{128,112},... | collective-permute-start | bytes 73736 | tf_op jit(solution)/shard_map/ppermute | solution.py:23
  479.2 26.9 %collective-permute-start.26 = (f32[3,18,1,64]{3,2,1,0:T(1,128)}, f32[3,18,1,64]{3,2,1,0:T(1,128)}, u32[]{:S(2)}, u32[]{:S(2)}) collective-permute-start(f32[3,18,1,64]{3,2,1,0:T(1,128)} %get-tuple-element.117), channel_id=1, source_target_pairs={{0,1},{1,2},{2,3},{3,4},{4,5},{5,6},{6,7},{7,8},{8,9},{9,10},{10,1... | collective-permute-start | bytes 41480 | tf_op jit(solution)/shard_map/ppermute | solution.py:21
  482.2 23.9 %collective-permute-start.27 = (f32[3,18,1,64]{3,2,1,0:T(1,128)}, f32[3,18,1,64]{3,2,1,0:T(1,128)}, u32[]{:S(2)}, u32[]{:S(2)}) collective-permute-start(f32[3,18,1,64]{3,2,1,0:T(1,128)} %get-tuple-element.118), channel_id=1, source_target_pairs={{1,0},{2,1},{3,2},{4,3},{5,4},{6,5},{7,6},{8,7},{9,8},{10,9},{11,1... | collective-permute-start | bytes 41480 | tf_op jit(solution)/shard_map/ppermute | solution.py:23
  536.7 91.9 %copy-start.131 = (f32[1,16,32,64]{3,2,1,0:T(8,128)S(1)}, f32[1,16,32,64]{3,2,1,0:T(8,128)}, u32[]{:S(2)}) copy-start(f32[1,16,32,64]{3,2,1,0:T(8,128)} %get-tuple-element.85) | copy-start | bytes 393220
  539.3 89.6 %copy-start.130 = (f32[1,16,32,64]{3,2,1,0:T(8,128)S(1)}, f32[1,16,32,64]{3,2,1,0:T(8,128)}, u32[]{:S(2)}) copy-start(f32[1,16,32,64]{3,2,1,0:T(8,128)} %get-tuple-element.131) | copy-start | bytes 393220
  539.3 89.8 %copy-start.129 = (f32[1,16,32,64]{3,2,1,0:T(8,128)S(1)}, f32[1,16,32,64]{3,2,1,0:T(8,128)}, u32[]{:S(2)}) copy-start(f32[1,16,32,64]{3,2,1,0:T(8,128)} %get-tuple-element.86) | copy-start | bytes 393220
  540.3 92.0 %copy-start.140 = (f32[1,16,2048]{2,1,0:T(8,128)S(1)}, f32[1,16,2048]{2,1,0:T(8,128)}, u32[]{:S(2)}) copy-start(f32[1,16,2048]{2,1,0:T(8,128)} %get-tuple-element.174) | copy-start | bytes 393220
  540.3 92.0 %copy-start.141 = (f32[1,16,2048]{2,1,0:T(8,128)S(1)}, f32[1,16,2048]{2,1,0:T(8,128)}, u32[]{:S(2)}) copy-start(f32[1,16,2048]{2,1,0:T(8,128)} %get-tuple-element.176) | copy-start | bytes 393220
  540.3 92.0 %copy-start.144 = (f32[1,16,2048]{2,1,0:T(8,128)S(1)}, f32[1,16,2048]{2,1,0:T(8,128)}, u32[]{:S(2)}) copy-start(f32[1,16,2048]{2,1,0:T(8,128)} %stack.119) | copy-start | bytes 393220
  540.3 92.0 %copy-start.145 = (f32[1,16,2048]{2,1,0:T(8,128)S(1)}, f32[1,16,2048]{2,1,0:T(8,128)}, u32[]{:S(2)}) copy-start(f32[1,16,2048]{2,1,0:T(8,128)} %stack.120) | copy-start | bytes 393220
  540.3 92.0 %copy-start.152 = (f32[1,16,2048]{2,1,0:T(8,128)S(1)}, f32[1,16,2048]{2,1,0:T(8,128)}, u32[]{:S(2)}) copy-start(f32[1,16,2048]{2,1,0:T(8,128)} %stack.121) | copy-start | bytes 393220
  540.3 92.0 %copy-start.153 = (f32[1,16,2048]{2,1,0:T(8,128)S(1)}, f32[1,16,2048]{2,1,0:T(8,128)}, u32[]{:S(2)}) copy-start(f32[1,16,2048]{2,1,0:T(8,128)} %stack.123) | copy-start | bytes 393220
  540.3 92.0 %copy-start.158 = (f32[1,16,2048]{2,1,0:T(8,128)S(1)}, f32[1,16,2048]{2,1,0:T(8,128)}, u32[]{:S(2)}) copy-start(f32[1,16,2048]{2,1,0:T(8,128)} %get-tuple-element.79) | copy-start | bytes 393220
  (178 other events, 1352.7 us)
